TPU v7x, 256 devices: a whole 4x4x8 slice. The times are simulated.
256 devices in a mesh: grp: 8 (over z), tp: 32 (over y, x, core).
Axes of the slice: x: 4, y: 4, z: 8, core: 2. Of those that a mesh axis runs over, the one named last changes fastest.
Arguments:
- hidden_in: bfloat16 [512, 4096], P('grp'), may hold values from -6 to 6
- norm_gain: float32 [4096], replicated, may hold values from 0.25 to 1.75
- head_weight: bfloat16 [4096, 128256], P('grp', 'tp'), may hold values from -1 to 1
- ffn_act: bfloat16 [512, 14336], P('grp', 'tp'), may hold values from -6 to 6
- labels: int32 [512], P('grp'), may hold values from 0 to 128255
- lengths: int32 [64], P('grp'), may hold values from 1 to 8
- proj_hidden: bfloat16 [4096, 64], replicated, may hold values from -0.09375 to 0.09375
- proj_vocab: bfloat16 [128256, 64], P('tp'), may hold values from -6 to 6
- proj_ffn: bfloat16 [14336, 64], P('tp'), may hold values from -0.046875 to 0.046875
- proj_down: bfloat16 [4096, 64], replicated, may hold values from -6 to 6
- store: bfloat16 [65536, 8192], P('grp', 'tp'), may hold values from -0.0625 to 0.0625
Outputs:
- scores: float32 [64, 65536], P('tp', 'grp')
All inputs are finite; a program needn't handle non-finite values.
Results may differ from a plain program's by a relative error of at most 0.012.
Values may be sent and summed in bfloat16 or wider, within the bound.
No kernel may reach another device: no remote copies, remote signals or barrier semaphores. Data moves between devices by JAX's collectives and lax.ppermute only.
A program may use at most 64 MiB of HBM per device.

v0:
```python
import jax
import jax.numpy as jnp
from jax import lax
from jax.sharding import PartitionSpec as P

epsilon = 1e-05
highest = lax.Precision.HIGHEST


def sent_to_all(value, axis):
    copies = jnp.broadcast_to(value, (lax.axis_size(axis), *value.shape))
    return lax.all_to_all(copies, axis, split_axis=0, concat_axis=0, tiled=True)


def over_copies(value, axis):
    everything = sent_to_all(value, axis)
    return jnp.max(everything, axis=0)


def of_everyone(value, axis):
    everything = sent_to_all(value, axis)
    return jnp.sum(everything, axis=0)


def packed_total(arrays, axis):
    vector, at, outs = (jnp.concatenate([a.reshape(-1) for a in arrays]), 0, [])
    so_far = of_everyone(vector, axis)
    for a in arrays:
        outs.append(so_far[at : at + a.size].reshape(a.shape))
        at += a.size
    return tuple(outs)


def laid_out(tiles, dim):
    shape = list(tiles.shape[1:])
    shape[dim] *= tiles.shape[0]
    return jnp.moveaxis(tiles, 0, dim).reshape(shape)


def gather_directly(value, axis, dim):
    tiles = sent_to_all(value, axis)
    return laid_out(tiles, dim)


def cut_along(value, dim, length):
    before, after = (value.shape[:dim], value.shape[dim + 1 :])
    return jnp.moveaxis(value.reshape(*before, length, -1, *after), dim, 0)


def sent_and_summed(value, axis, dim):
    tiles = cut_along(value, dim, lax.axis_size(axis))
    arrived = lax.all_to_all(tiles, axis, split_axis=0, concat_axis=0, tiled=True)
    return arrived.sum(axis=0)


def fold_rows(pieces, high_part, low_part):
    contract = (((0,), (0,)), ((), ()))
    upper = lax.dot_general(pieces, high_part, contract, preferred_element_type=jnp.float32)
    return upper + lax.dot_general(pieces, low_part, contract, preferred_element_type=jnp.float32)


def per_device(
    hidden_in,
    norm_gain,
    head_weight,
    ffn_act,
    labels,
    lengths,
    proj_hidden,
    proj_vocab,
    proj_ffn,
    proj_down,
    store,
):
    token_count, model_width = hidden_in.shape
    query_here = lengths.shape[0]
    seq_span = token_count // query_here
    rows_owned, vocab_owned = head_weight.shape
    rank_size = proj_hidden.shape[1]
    group_index = lax.axis_index("grp")
    vocab_index = lax.axis_index("tp")
    wide_hidden = hidden_in.astype(jnp.float32)
    inverse = lax.rsqrt(jnp.mean(wide_hidden * wide_hidden, axis=1, keepdims=True) + epsilon)
    unit_hidden = wide_hidden * inverse
    normed = (norm_gain * unit_hidden).astype(jnp.bfloat16)
    gained_down = norm_gain[:, None] * proj_down.astype(jnp.float32)
    down_high = gained_down.astype(jnp.bfloat16)
    down_low = (gained_down - down_high.astype(jnp.float32)).astype(jnp.bfloat16)
    spread = lax.all_to_all(normed, "grp", split_axis=1, concat_axis=0, tiled=True)
    logits = lax.psum_scatter(
        jnp.dot(spread, head_weight, preferred_element_type=jnp.float32),
        "grp",
        scatter_dimension=0,
        tiled=True,
    )
    local_max = jnp.max(logits, axis=1)
    peak = over_copies(local_max, "tp")
    denominator = of_everyone(jnp.sum(jnp.exp(logits - peak[:, None]), axis=1), "tp")
    probs = jnp.exp(logits - peak[:, None]) / denominator[:, None]
    positions = lax.broadcasted_iota(jnp.int32, (token_count,), 0) % seq_span
    valid = positions < jnp.repeat(lengths, seq_span)
    vocab_ids = vocab_index * vocab_owned + lax.broadcasted_iota(jnp.int32, (1, vocab_owned), 1)
    onehot = (labels[:, None] == vocab_ids).astype(jnp.float32)
    grads = jnp.where(valid[:, None], probs - onehot, 0.0).astype(jnp.bfloat16)
    own_high = lax.dynamic_slice_in_dim(down_high, group_index * rows_owned, rows_owned, 0)
    own_low = lax.dynamic_slice_in_dim(down_low, group_index * rows_owned, rows_owned, 0)
    local_fold = fold_rows(head_weight, own_high, own_low)
    folded_sum = lax.psum(local_fold, "grp")
    down_sum = jnp.dot(grads.astype(jnp.float32), folded_sum, precision=highest)
    head_side = jnp.dot(grads, proj_vocab, preferred_element_type=jnp.float32)
    label_dot = jnp.sum(grads.astype(jnp.float32) * logits, axis=1)
    ffn_side = jnp.dot(ffn_act, proj_ffn, preferred_element_type=jnp.float32)
    head_side, down_sum, label_dot, ffn_side = packed_total(
        (head_side, down_sum, label_dot, ffn_side), "tp"
    )
    hidden_side = jnp.dot(normed, proj_hidden, preferred_element_type=jnp.float32)
    unit_down = jnp.dot(unit_hidden, proj_down.astype(jnp.float32), precision=highest)
    down_side = inverse * (down_sum - (label_dot / model_width)[:, None] * unit_down)
    shaped = (query_here, seq_span, rank_size)
    first_outer = jnp.einsum("spa,spb->sab", hidden_side.reshape(shaped), head_side.reshape(shaped))
    second_outer = jnp.einsum("spa,spb->sab", ffn_side.reshape(shaped), down_side.reshape(shaped))
    queries = jnp.concatenate(
        [first_outer.reshape(query_here, -1), second_outer.reshape(query_here, -1)], axis=1
    ).astype(jnp.bfloat16)
    feature_owned = store.shape[1]
    own_queries = lax.dynamic_slice_in_dim(queries, vocab_index * feature_owned, feature_owned, 1)
    every_query = gather_directly(own_queries, "grp", 0)
    return sent_and_summed(
        lax.dot_general(
            every_query, store, (((1,), (1,)), ((), ())), preferred_element_type=jnp.float32
        ),
        "tp",
        0,
    )


def solution(mesh):
    return jax.shard_map(
        per_device,
        mesh=mesh,
        in_specs=(
            P("grp", None),
            P(),
            P("grp", "tp"),
            P("grp", "tp"),
            P("grp"),
            P("grp"),
            P(),
            P("tp", None),
            P("tp", None),
            P(),
            P("grp", "tp"),
        ),
        out_specs=P("tp", "grp"),
        check_vma=False,
    )
```

profile of v0, /device:TPU:1, one launch (start us, length us, event | category | flops | bytes accessed | tf_op | source)
XLA Modules:
  0.0 308.6 jit_solution(2016261024021584329)
XLA Ops:
  6.5 0.0 copy-start
  6.5 0.0 reduce-scatter.2.cloned.1.call-start
  6.5 1.3 fusion.10
  7.9 1.2 fusion.9
  9.1 24.9 %all_to_all.47 = bf16[64,8,512]{2,0,1:T(8,128)(2,1)S(1)} all-to-all(bf16[64,8,512]{2,0,1:T(8,128)(2,1)S(1)} %bitcast.38), channel_id=1, replica_groups=mesh['grp'=8,'tp'=32] {'grp'}, dimensions={1} | all-to-all | bytes 1048576 | tf_op jit(solution)/shard_map/all_to_all | solution.py:89
  34.1 7.8 %fusion.25 = f32[512,4008]{1,0:T(8,128)} fusion(bf16[512,512]{1,0:T(8,128)(2,1)S(1)} %bitcast.37, bf16[512,4008]{0,1:T(8,128)(2,1)} %param.13), kind=kOutput, calls=%fused_computation.42 | convolution fusion | flops 2101346304 | bytes 12836864 | tf_op jit(solution)/shard_map/dot_general | solution.py:91
  41.9 0.0 reduce-scatter.2.cloned.1.call-update
  41.9 0.0 all-reduce.2.cloned.1.call-start
  42.0 1.0 copy-done.3
  42.9 0.0 copy-done.5
  42.9 0.1 convert_multiply_fusion.11
  43.1 3.7 %fusion.17 = f32[64,4008]{1,0:T(8,128)S(1)} fusion(bf16[512,4008]{0,1:T(8,128)(2,1)} %param.13, bf16[4096,64]{0,1:T(8,128)(2,1)S(1)} %get-tuple-element.8, s32[]{:T(128)S(6)} %select_n.24), kind=kOutput, calls=%fused_computation.30 | convolution fusion | flops 262668288 | bytes 5195780 | tf_op jit(solution)/shard_map/dot_general | solution.py:58
  46.7 0.0 copy-start.9
  46.7 0.0 copy-start.6
  46.8 0.0 copy-start.7
  46.8 0.0 copy-done.1
  46.8 0.0 copy-start.8
  46.8 2.3 fusion
  49.1 0.0 all-reduce.2.cloned.1.call-update
  49.2 0.0 copy-done.9
  49.2 0.1 broadcast_in_dim.36
  49.2 0.1 reshape.90
  49.3 0.0 copy-done.6
  49.3 0.0 copy-done.7
  49.3 0.2 fusion.28
  49.5 85.5 %reduce-scatter.2.cloned.1.call-done = f32[64,4008]{1,0:T(8,128)} async-done(((f32[512,4008]{1,0:T(8,128)}), f32[64,4008]{1,0:T(8,128)}) %reduce-scatter.2.cloned.1.call-update) | async-done | bytes 1026064 | tf_op jit(solution)/shard_map/reduce_scatter | solution.py:90
  134.9 1.4 reduce_max.18
  136.3 0.6 broadcast_in_dim.38
  136.9 7.6 %all-to-all-start.1 = ((f32[32,1,64]{2,1,0:T(1,128)}), f32[32,1,64]{2,1,0:T(1,128)S(1)}, u32[]{:S(2)}, u32[]{:S(2)}) async-start(f32[32,1,64]{2,1,0:T(1,128)} %broadcast_in_dim.38), calls=%async_computation.2 | async-start | bytes 32768 | tf_op jit(solution)/shard_map/all_to_all | solution.py:12
  144.5 6.9 %all-to-all-done.1 = f32[32,1,64]{2,1,0:T(1,128)S(1)} async-done(((f32[32,1,64]{2,1,0:T(1,128)}), f32[32,1,64]{2,1,0:T(1,128)S(1)}, u32[]{:S(2)}, u32[]{:S(2)}) %all-to-all-start.1) | async-done | bytes 8224 | tf_op jit(solution)/shard_map/all_to_all | solution.py:12
  151.4 1.5 fusion.11
  153.0 0.6 broadcast_in_dim.39
  153.6 4.1 %all-to-all-start.2 = ((f32[32,1,64]{2,1,0:T(1,128)}), f32[32,1,64]{2,1,0:T(1,128)S(1)}, u32[]{:S(2)}, u32[]{:S(2)}) async-start(f32[32,1,64]{2,1,0:T(1,128)} %broadcast_in_dim.39), calls=%async_computation.3 | async-start | bytes 32768 | tf_op jit(solution)/shard_map/all_to_all | solution.py:12
  157.8 0.1 reshape.93
  157.8 6.9 %all-to-all-done.2 = f32[32,1,64]{2,1,0:T(1,128)S(1)} async-done(((f32[32,1,64]{2,1,0:T(1,128)}), f32[32,1,64]{2,1,0:T(1,128)S(1)}, u32[]{:S(2)}, u32[]{:S(2)}) %all-to-all-start.2) | async-done | bytes 8224 | tf_op jit(solution)/shard_map/all_to_all | solution.py:12
  164.8 0.0 copy-done.8
  164.8 1.8 multiply_reduce_fusion
  166.6 0.0 copy-done.4
  166.6 0.3 fusion.26
  166.9 0.1 reshape.91
  166.9 40.7 %all-reduce.2.cloned.1.call-done = f32[4008,64]{0,1:T(8,128)} async-done(((f32[4008,64]{0,1:T(8,128)}), f32[4008,64]{0,1:T(8,128)}) %all-reduce.2.cloned.1.call-update) | async-done | bytes 1026064 | tf_op jit(solution)/shard_map/psum | solution.py:108
  207.6 1.9 fusion.27
  209.5 0.0 copy-start.2
  209.5 0.1 reshape.92
  209.6 0.1 concatenate.7
  209.7 2.0 broadcast_in_dim.41
  211.6 11.9 %all-to-all-start.3 = ((f32[32,1,12352]{2,1,0:T(1,128)}), f32[32,1,12352]{2,1,0:T(1,128)S(1)}, u32[]{:S(2)}, u32[]{:S(2)}) async-start(f32[32,1,12352]{2,1,0:T(1,128)} %broadcast_in_dim.41), calls=%async_computation.4 | async-start | bytes 3178496 | tf_op jit(solution)/shard_map/all_to_all | solution.py:12
  223.6 22.4 %all-to-all-done.3 = f32[32,1,12352]{2,1,0:T(1,128)S(1)} async-done(((f32[32,1,12352]{2,1,0:T(1,128)}), f32[32,1,12352]{2,1,0:T(1,128)S(1)}, u32[]{:S(2)}, u32[]{:S(2)}) %all-to-all-start.3) | async-done | bytes 1581088 | tf_op jit(solution)/shard_map/all_to_all | solution.py:12
  246.0 0.9 reduce_sum.58
  246.9 0.1 fusion.24
  247.0 0.1 reshape_reshape.6
  247.1 0.0 copy-done
  247.1 0.6 convolution_convert_fusion.1
  247.7 0.2 reshape.94
  247.9 0.1 reshape_reshape.7
  248.0 0.1 reshape.95
  248.0 1.8 fusion.8
  249.8 0.2 fusion.29
  250.0 0.2 reshape.97
  250.3 10.6 %all_to_all.48 = bf16[8,8,256]{2,1,0:T(8,128)(2,1)S(1)} all-to-all(bf16[8,8,256]{2,1,0:T(8,128)(2,1)S(1)} %broadcast_in_dim.42), channel_id=1, replica_groups=mesh['grp'=8,'tp'=32] {'grp'}, dimensions={0} | all-to-all | bytes 65536 | tf_op jit(solution)/shard_map/all_to_all | solution.py:12
  260.8 3.6 %fusion.1 = f32[32,2,8192]{2,0,1:T(8,128)S(1)} fusion(bf16[8192,256]{1,0:T(8,128)(2,1)} %param.21, bf16[32,2,256]{2,1,0:T(2,128)(2,1)S(1)} %dot_general.45), kind=kOutput, calls=%fused_computation.2 | convolution fusion | flops 268435456 | bytes 6324224 | tf_op jit(solution)/shard_map/dot_general | solution.py:129
  264.4 1.6 copy.26
  266.0 34.4 %all_to_all.49 = f32[32,2,8192]{2,1,0:T(2,128)S(1)} all-to-all(f32[32,2,8192]{2,1,0:T(2,128)S(1)} %copy.26), channel_id=1, replica_groups=mesh['grp'=8,'tp'=32] {'tp'}, dimensions={0} | all-to-all | bytes 4194304 | tf_op jit(solution)/shard_map/all_to_all | solution.py:52
  300.4 1.4 reduce_sum.59
  (16 shorter events, 0.2 us)
Async XLA Ops:
  6.5 240.6 %copy-start = (bf16[4096,64]{0,1:T(8,128)(2,1)S(1)}, bf16[4096,64]{0,1:T(8,128)(2,1)}, u32[]{:S(2)}) copy-start(bf16[4096,64]{0,1:T(8,128)(2,1)} %param.17) | copy-start | bytes 1572868
  6.5 128.4 %reduce-scatter.2.cloned.1.call-start = ((), (), s32[]{:S(2)}) async-start(), calls=%async_computation.7 | async-start | bytes 9437184 | tf_op jit(solution)/shard_map/reduce_scatter | solution.py:90
  41.9 1.0 copy-start.3
  41.9 1.0 copy-start.5
  41.9 165.7 %all-reduce.2.cloned.1.call-start = ((), (), s32[]{:S(2)}) async-start(), calls=%async_computation.8 | async-start | bytes 2097152 | tf_op jit(solution)/shard_map/psum | solution.py:108
  42.9 3.9 %copy-start.1 = (bf16[512,4008]{0,1:T(8,128)(2,1)S(1)}, bf16[512,4008]{0,1:T(8,128)(2,1)}, u32[]{:S(2)}) copy-start(bf16[512,4008]{0,1:T(8,128)(2,1)} %param.13) | copy-start | bytes 12312580
  46.7 2.4 copy-start.9
  46.7 2.6 copy-start.6
  46.8 2.6 copy-start.7
  46.8 118.0 %copy-start.8 = (s32[64]{0:T(128)S(1)}, s32[64]{0:T(128)}, u32[]{:S(2)}) copy-start(s32[64]{0:T(128)} %param.15) | copy-start | bytes 772
  49.1 117.4 %copy-start.4 = (bf16[4008,64]{0,1:T(8,128)(2,1)S(1)}, bf16[4008,64]{0,1:T(8,128)(2,1)}, u32[]{:S(2)}) copy-start(bf16[4008,64]{0,1:T(8,128)(2,1)} %param.18) | copy-start | bytes 1539076
  136.9 14.5 %all-to-all-start.1 = ((f32[32,1,64]{2,1,0:T(1,128)}), f32[32,1,64]{2,1,0:T(1,128)S(1)}, u32[]{:S(2)}, u32[]{:S(2)}) async-start(f32[32,1,64]{2,1,0:T(1,128)} %broadcast_in_dim.38), calls=%async_computation.2 | async-start | bytes 32768 | tf_op jit(solution)/shard_map/all_to_all | solution.py:12
  153.6 11.1 %all-to-all-start.2 = ((f32[32,1,64]{2,1,0:T(1,128)}), f32[32,1,64]{2,1,0:T(1,128)S(1)}, u32[]{:S(2)}, u32[]{:S(2)}) async-start(f32[32,1,64]{2,1,0:T(1,128)} %broadcast_in_dim.39), calls=%async_computation.3 | async-start | bytes 32768 | tf_op jit(solution)/shard_map/all_to_all | solution.py:12
  209.5 38.5 %copy-start.2 = (bf16[64,4096]{1,0:T(8,128)(2,1)S(1)}, bf16[64,4096]{1,0:T(8,128)(2,1)}, u32[]{:S(2)}) copy-start(bf16[64,4096]{1,0:T(8,128)(2,1)} %param.11) | copy-start | bytes 1572868
  211.6 34.4 %all-to-all-start.3 = ((f32[32,1,12352]{2,1,0:T(1,128)}), f32[32,1,12352]{2,1,0:T(1,128)S(1)}, u32[]{:S(2)}, u32[]{:S(2)}) async-start(f32[32,1,12352]{2,1,0:T(1,128)} %broadcast_in_dim.41), calls=%async_computation.4 | async-start | bytes 3178496 | tf_op jit(solution)/shard_map/all_to_all | solution.py:12
Sparse Core Ops, SparseCore 0:
  42.0 92.8 reduce-scatter.1
  137.3 70.2 all-reduce.1
where the time goes:
time: 309 us
  waiting for transfers between devices  162 us (52%)
  blocking collectives  69.8 us (23%)
  starting transfers between devices  23.7 us (8%)
  matrix products  22.3 us (7%)
  between operations  13.7 us (4%)
  other arithmetic  9.72 us (3%)
  local copies, waits for them, and re-layouts  7.04 us (2%)
    reduce_scatter x1, waiting for transfers between devices, per_device(): lax.psum_scatter(jnp.dot(spread, head_weight, preferred_element_type=jnp....  85.5 us
    psum x1, waiting for transfers between devices, per_device(): folded_sum = lax.psum(local_fold, 'grp')  40.7 us
    all_to_all x3, waiting for transfers between devices, sent_to_all(): return lax.all_to_all(copies, axis, split_axis=0, concat_axis=0, tiled=True)  36.2 us
    all_to_all x1, blocking collectives, sent_and_summed(): lax.all_to_all(tiles, axis, split_axis=0, concat_axis=0, tiled=True)  34.4 us
    all_to_all x1, blocking collectives, per_device(): lax.all_to_all(normed, 'grp', split_axis=1, concat_axis=0, tiled=True)  24.9 us
    all_to_all x3, starting transfers between devices, sent_to_all(): return lax.all_to_all(copies, axis, split_axis=0, concat_axis=0, tiled=True)  23.6 us
    all_to_all x1, blocking collectives, sent_to_all(): return lax.all_to_all(copies, axis, split_axis=0, concat_axis=0, tiled=True)  10.6 us
    dot_general x1, matrix products, per_device(): jnp.dot(spread, head_weight, preferred_element_type=jnp.float32)  7.81 us
  transfers between devices with their start and end apart: 5, of which 5 were waited for; matrix products, arithmetic and copies ran while one was open for 4% of the time, Pallas kernels for 0%

commit v1 on v0

--- a/solution.py
+++ b/solution.py
@@ -2,9 +2,19 @@
 import jax.numpy as jnp
 from jax import lax
 from jax.sharding import PartitionSpec as P
+from jax.lax import axis_size, ppermute
 
 epsilon = 1e-05
 highest = lax.Precision.HIGHEST
+
+
+def _meet_ports(inner_x):
+    how_many = axis_size("grp")
+    vec_out = lambda y2: [(k, k ^ y2) for k in range(how_many)]
+    g_now = inner_x
+    for j in range(how_many.bit_length() - 1):
+        g_now = g_now + ppermute(g_now, "grp", vec_out(1 << j))
+    return g_now
 
 
 def sent_to_all(value, axis):
@@ -105,7 +115,7 @@
     own_high = lax.dynamic_slice_in_dim(down_high, group_index * rows_owned, rows_owned, 0)
     own_low = lax.dynamic_slice_in_dim(down_low, group_index * rows_owned, rows_owned, 0)
     local_fold = fold_rows(head_weight, own_high, own_low)
-    folded_sum = lax.psum(local_fold, "grp")
+    folded_sum = _meet_ports(local_fold)
     down_sum = jnp.dot(grads.astype(jnp.float32), folded_sum, precision=highest)
     head_side = jnp.dot(grads, proj_vocab, preferred_element_type=jnp.float32)
     label_dot = jnp.sum(grads.astype(jnp.float32) * logits, axis=1)

time: 309 us -> 362 us (1.17)
  waiting for transfers between devices: 162 us -> 206 us
  blocking collectives: 69.8 us -> 79.8 us
    ppermute x0 -> x3, waiting for transfers between devices: none -> 107 us  [_meet_ports(): g_now = g_now + ppermute(g_now, 'grp', vec_out(1 << j))]
    psum x1 -> x0, waiting for transfers between devices: 40.7 us -> none  [per_device(): folded_sum = lax.psum(local_fold, 'grp')]
    reduce_scatter x1, waiting for transfers between devices: 85.5 us -> 63.2 us  [per_device(): lax.psum_scatter(jnp.dot(spread, head_weight, preferred_element_type=jnp....]
    all_to_all x1, blocking collectives: 10.6 us -> 20.5 us  [sent_to_all(): return lax.all_to_all(copies, axis, split_axis=0, concat_axis=0, tiled=True)]
    all_to_all x3, starting transfers between devices: 23.6 us -> 16.8 us  [sent_to_all(): return lax.all_to_all(copies, axis, split_axis=0, concat_axis=0, tiled=True)]
    ppermute x0 -> x3, starting transfers between devices: none -> 3.85 us  [_meet_ports(): g_now = g_now + ppermute(g_now, 'grp', vec_out(1 << j))]
  transfers between devices with their start and end apart: 5 -> 7, of which waited for: 5 -> 6; matrix products, arithmetic and copies ran while one was open for 4% -> 4% of each run, Pallas kernels for 0% -> 0%
where the time goes in v1:
time: 362 us; the launch traced here: 361 us
  waiting for transfers between devices  206 us (57%)
  blocking collectives  79.8 us (22%)
  matrix products  22.3 us (6%)
  starting transfers between devices  20.7 us (6%)
  between operations  13.7 us (4%)
  other arithmetic  11.2 us (3%)
  local copies, waits for them, and re-layouts  7.09 us (2%)
    ppermute x3, waiting for transfers between devices, _meet_ports(): g_now = g_now + ppermute(g_now, 'grp', vec_out(1 << j))  107 us
    reduce_scatter x1, waiting for transfers between devices, per_device(): lax.psum_scatter(jnp.dot(spread, head_weight, preferred_element_type=jnp....  63.2 us
    all_to_all x3, waiting for transfers between devices, sent_to_all(): return lax.all_to_all(copies, axis, split_axis=0, concat_axis=0, tiled=True)  36.3 us
    all_to_all x1, blocking collectives, sent_and_summed(): lax.all_to_all(tiles, axis, split_axis=0, concat_axis=0, tiled=True)  34.4 us
    all_to_all x1, blocking collectives, per_device(): lax.all_to_all(normed, 'grp', split_axis=1, concat_axis=0, tiled=True)  24.9 us
    all_to_all x1, blocking collectives, sent_to_all(): return lax.all_to_all(copies, axis, split_axis=0, concat_axis=0, tiled=True)  20.5 us
    all_to_all x3, starting transfers between devices, sent_to_all(): return lax.all_to_all(copies, axis, split_axis=0, concat_axis=0, tiled=True)  16.8 us
    dot_general x1, matrix products, per_device(): jnp.dot(spread, head_weight, preferred_element_type=jnp.float32)  7.81 us
  transfers between devices with their start and end apart: 7, of which 6 were waited for; matrix products, arithmetic and copies ran while one was open for 4% of the time, Pallas kernels for 0%

profile of v1, /device:TPU:1, one launch (start us, length us, event | category | flops | bytes accessed | tf_op | source)
XLA Modules:
  0.0 361.1 jit_solution(4116357961379938424)
XLA Ops:
  6.5 0.0 copy-start
  6.5 0.0 reduce-scatter.2.cloned.1.call-start
  6.5 1.3 fusion.10
  7.9 1.2 fusion.9
  9.1 24.9 %all_to_all.47 = bf16[64,8,512]{2,0,1:T(8,128)(2,1)S(1)} all-to-all(bf16[64,8,512]{2,0,1:T(8,128)(2,1)S(1)} %bitcast.37), channel_id=1, replica_groups=mesh['grp'=8,'tp'=32] {'grp'}, dimensions={1} | all-to-all | bytes 1048576 | tf_op jit(solution)/shard_map/all_to_all | solution.py:99
  34.1 7.8 %fusion.27 = f32[512,4008]{1,0:T(8,128)} fusion(bf16[512,512]{1,0:T(8,128)(2,1)S(1)} %bitcast.36, bf16[512,4008]{0,1:T(8,128)(2,1)} %param.13), kind=kOutput, calls=%fused_computation.44 | convolution fusion | flops 2101346304 | bytes 12836864 | tf_op jit(solution)/shard_map/dot_general | solution.py:101
  41.9 0.0 reduce-scatter.2.cloned.1.call-update
  41.9 1.0 copy-done.3
  42.9 0.0 copy-done.4
  42.9 0.1 convert_multiply_fusion.11
  43.1 3.7 %fusion.19 = f32[64,4008]{1,0:T(8,128)S(1)} fusion(bf16[512,4008]{0,1:T(8,128)(2,1)} %param.13, bf16[4096,64]{0,1:T(8,128)(2,1)S(1)} %get-tuple-element.8, s32[]{:T(128)S(6)} %select_n.24), kind=kOutput, calls=%fused_computation.32 | convolution fusion | flops 262668288 | bytes 5195780 | tf_op jit(solution)/shard_map/dot_general | solution.py:68
  46.7 0.0 copy-done.1
  46.7 0.0 copy-start.8
  46.8 0.0 copy-start.5
  46.8 0.0 copy-start.6
  46.8 1.4 fusion
  48.1 0.0 copy-start.7
  48.2 0.1 collective-permute-start
  48.3 40.1 %collective-permute-done = f32[4008,64]{0,1:T(8,128)S(1)} collective-permute-done((f32[4008,64]{0,1:T(8,128)S(1)}, f32[4008,64]{0,1:T(8,128)S(1)}, u32[]{:S(2)}, u32[]{:S(2)}) %collective-permute-start) | collective-permute-done | bytes 1026080 | tf_op jit(solution)/shard_map/ppermute | solution.py:16
  88.4 0.2 add.64
  88.6 0.1 collective-permute-start.1
  88.7 0.0 copy-done.8
  88.7 0.1 broadcast_in_dim.36
  88.8 0.1 reshape.90
  88.8 0.2 fusion.29
  89.0 66.6 %collective-permute-done.1 = f32[4008,64]{0,1:T(8,128)} collective-permute-done((f32[4008,64]{0,1:T(8,128)S(1)}, f32[4008,64]{0,1:T(8,128)}, u32[]{:S(2)}, u32[]{:S(2)}) %collective-permute-start.1) | collective-permute-done | bytes 1026080 | tf_op jit(solution)/shard_map/ppermute | solution.py:16
  155.6 1.3 add.65
  156.9 3.7 %collective-permute-start.2 = (f32[4008,64]{0,1:T(8,128)S(1)}, f32[4008,64]{0,1:T(8,128)}, u32[]{:S(2)}, u32[]{:S(2)}) collective-permute-start(f32[4008,64]{0,1:T(8,128)S(1)} %add.65), channel_id=1, source_target_pairs={{0,128},{32,160},{64,192},{96,224},{128,0},{160,32},{192,64},{224,... | collective-permute-start | bytes 3078152 | tf_op jit(solution)/shard_map/ppermute | solution.py:16
  160.6 63.2 %reduce-scatter.2.cloned.1.call-done = f32[64,4008]{1,0:T(8,128)} async-done(((f32[512,4008]{1,0:T(8,128)}), f32[64,4008]{1,0:T(8,128)}) %reduce-scatter.2.cloned.1.call-update) | async-done | bytes 1026064 | tf_op jit(solution)/shard_map/reduce_scatter | solution.py:100
  223.7 1.4 reduce_max.18
  225.1 0.6 broadcast_in_dim.38
  225.7 8.4 %all-to-all-start.1 = ((f32[32,1,64]{2,1,0:T(1,128)}), f32[32,1,64]{2,1,0:T(1,128)S(1)}, u32[]{:S(2)}, u32[]{:S(2)}) async-start(f32[32,1,64]{2,1,0:T(1,128)} %broadcast_in_dim.38), calls=%async_computation.2 | async-start | bytes 32768 | tf_op jit(solution)/shard_map/all_to_all | solution.py:22
  234.2 6.9 %all-to-all-done.1 = f32[32,1,64]{2,1,0:T(1,128)S(1)} async-done(((f32[32,1,64]{2,1,0:T(1,128)}), f32[32,1,64]{2,1,0:T(1,128)S(1)}, u32[]{:S(2)}, u32[]{:S(2)}) %all-to-all-start.1) | async-done | bytes 8224 | tf_op jit(solution)/shard_map/all_to_all | solution.py:22
  241.1 1.5 fusion.13
  242.6 0.6 broadcast_in_dim.39
  243.3 4.1 %all-to-all-start.2 = ((f32[32,1,64]{2,1,0:T(1,128)}), f32[32,1,64]{2,1,0:T(1,128)S(1)}, u32[]{:S(2)}, u32[]{:S(2)}) async-start(f32[32,1,64]{2,1,0:T(1,128)} %broadcast_in_dim.39), calls=%async_computation.3 | async-start | bytes 32768 | tf_op jit(solution)/shard_map/all_to_all | solution.py:22
  247.4 0.1 reshape.93
  247.5 6.9 %all-to-all-done.2 = f32[32,1,64]{2,1,0:T(1,128)S(1)} async-done(((f32[32,1,64]{2,1,0:T(1,128)}), f32[32,1,64]{2,1,0:T(1,128)S(1)}, u32[]{:S(2)}, u32[]{:S(2)}) %all-to-all-start.2) | async-done | bytes 8224 | tf_op jit(solution)/shard_map/all_to_all | solution.py:22
  254.4 1.8 multiply_reduce_fusion
  256.2 1.3 fusion.28
  257.5 0.1 reshape.91
  257.6 0.0 collective-permute-done.2
  257.6 1.9 fusion.11
  259.5 0.0 copy-start.2
  259.5 0.1 reshape.92
  259.6 0.1 concatenate.7
  259.7 2.0 broadcast_in_dim.41
  261.7 4.3 %all-to-all-start.3 = ((f32[32,1,12352]{2,1,0:T(1,128)}), f32[32,1,12352]{2,1,0:T(1,128)S(1)}, u32[]{:S(2)}, u32[]{:S(2)}) async-start(f32[32,1,12352]{2,1,0:T(1,128)} %broadcast_in_dim.41), calls=%async_computation.4 | async-start | bytes 3178496 | tf_op jit(solution)/shard_map/all_to_all | solution.py:22
  266.0 22.5 %all-to-all-done.3 = f32[32,1,12352]{2,1,0:T(1,128)S(1)} async-done(((f32[32,1,12352]{2,1,0:T(1,128)}), f32[32,1,12352]{2,1,0:T(1,128)S(1)}, u32[]{:S(2)}, u32[]{:S(2)}) %all-to-all-start.3) | async-done | bytes 1581088 | tf_op jit(solution)/shard_map/all_to_all | solution.py:22
  288.5 0.9 reduce_sum.58
  289.4 0.1 fusion.26
  289.5 0.1 reshape_reshape.6
  289.5 0.6 convolution_convert_fusion.1
  290.1 0.2 reshape.94
  290.3 0.1 reshape_reshape.7
  290.4 0.1 reshape.95
  290.5 1.8 fusion.8
  292.2 0.2 fusion.30
  292.5 0.2 reshape.97
  292.7 20.5 %all_to_all.48 = bf16[8,8,256]{2,1,0:T(8,128)(2,1)S(1)} all-to-all(bf16[8,8,256]{2,1,0:T(8,128)(2,1)S(1)} %broadcast_in_dim.42), channel_id=1, replica_groups=mesh['grp'=8,'tp'=32] {'grp'}, dimensions={0} | all-to-all | bytes 65536 | tf_op jit(solution)/shard_map/all_to_all | solution.py:22
  313.2 3.6 fusion.1
  316.8 1.6 copy.26
  318.4 34.4 %all_to_all.49 = f32[32,2,8192]{2,1,0:T(2,128)S(1)} all-to-all(f32[32,2,8192]{2,1,0:T(2,128)S(1)} %copy.26), channel_id=1, replica_groups=mesh['grp'=8,'tp'=32] {'tp'}, dimensions={0} | all-to-all | bytes 4194304 | tf_op jit(solution)/shard_map/all_to_all | solution.py:62
  352.8 1.4 reduce_sum.59
  (19 shorter events, 0.2 us)
Async XLA Ops:
  6.5 283.0 %copy-start = (bf16[4096,64]{0,1:T(8,128)(2,1)S(1)}, bf16[4096,64]{0,1:T(8,128)(2,1)}, u32[]{:S(2)}) copy-start(bf16[4096,64]{0,1:T(8,128)(2,1)} %param.17) | copy-start | bytes 1572868
  6.5 217.2 %reduce-scatter.2.cloned.1.call-start = ((), (), s32[]{:S(2)}) async-start(), calls=%async_computation.7 | async-start | bytes 9437184 | tf_op jit(solution)/shard_map/reduce_scatter | solution.py:100
  41.9 1.0 copy-start.3
  41.9 1.0 copy-start.4
  42.9 3.8 %copy-start.1 = (bf16[512,4008]{0,1:T(8,128)(2,1)S(1)}, bf16[512,4008]{0,1:T(8,128)(2,1)}, u32[]{:S(2)}) copy-start(bf16[512,4008]{0,1:T(8,128)(2,1)} %param.13) | copy-start | bytes 12312580
  46.7 41.9 %copy-start.8 = (s32[8]{0:T(128)S(1)}, s32[8]{0:T(128)}, u32[]{:S(2)}) copy-start(s32[8]{0:T(128)} %param.16) | copy-start | bytes 100
  46.8 42.1 %copy-start.5 = (bf16[64,448]{1,0:T(8,128)(2,1)S(1)}, bf16[64,448]{1,0:T(8,128)(2,1)}, u32[]{:S(2)}) copy-start(bf16[64,448]{1,0:T(8,128)(2,1)} %param.14) | copy-start | bytes 172036
  46.8 42.1 %copy-start.6 = (bf16[448,64]{0,1:T(8,128)(2,1)S(1)}, bf16[448,64]{0,1:T(8,128)(2,1)}, u32[]{:S(2)}) copy-start(bf16[448,64]{0,1:T(8,128)(2,1)} %param.19) | copy-start | bytes 172036
  48.1 206.3 %copy-start.7 = (s32[64]{0:T(128)S(1)}, s32[64]{0:T(128)}, u32[]{:S(2)}) copy-start(s32[64]{0:T(128)} %param.15) | copy-start | bytes 772
  48.2 40.2 %collective-permute-start = (f32[4008,64]{0,1:T(8,128)S(1)}, f32[4008,64]{0,1:T(8,128)S(1)}, u32[]{:S(2)}, u32[]{:S(2)}) collective-permute-start(f32[4008,64]{0,1:T(8,128)S(1)} %fusion), channel_id=1, source_target_pairs={{0,32},{32,0},{64,96},{96,64},{128,160},{160,128},{192,224},{224,1... | collective-permute-start | bytes 3078152 | tf_op jit(solution)/shard_map/ppermute | solution.py:16
  88.6 67.0 %collective-permute-start.1 = (f32[4008,64]{0,1:T(8,128)S(1)}, f32[4008,64]{0,1:T(8,128)}, u32[]{:S(2)}, u32[]{:S(2)}) collective-permute-start(f32[4008,64]{0,1:T(8,128)S(1)} %add.64), channel_id=1, source_target_pairs={{0,64},{32,96},{64,0},{96,32},{128,192},{160,224},{192,128},{224,1... | collective-permute-start | bytes 3078152 | tf_op jit(solution)/shard_map/ppermute | solution.py:16
  156.9 100.7 %collective-permute-start.2 = (f32[4008,64]{0,1:T(8,128)S(1)}, f32[4008,64]{0,1:T(8,128)}, u32[]{:S(2)}, u32[]{:S(2)}) collective-permute-start(f32[4008,64]{0,1:T(8,128)S(1)} %add.65), channel_id=1, source_target_pairs={{0,128},{32,160},{64,192},{96,224},{128,0},{160,32},{192,64},{224,... | collective-permute-start | bytes 3078152 | tf_op jit(solution)/shard_map/ppermute | solution.py:16
  225.7 15.3 %all-to-all-start.1 = ((f32[32,1,64]{2,1,0:T(1,128)}), f32[32,1,64]{2,1,0:T(1,128)S(1)}, u32[]{:S(2)}, u32[]{:S(2)}) async-start(f32[32,1,64]{2,1,0:T(1,128)} %broadcast_in_dim.38), calls=%async_computation.2 | async-start | bytes 32768 | tf_op jit(solution)/shard_map/all_to_all | solution.py:22
  243.3 11.1 %all-to-all-start.2 = ((f32[32,1,64]{2,1,0:T(1,128)}), f32[32,1,64]{2,1,0:T(1,128)S(1)}, u32[]{:S(2)}, u32[]{:S(2)}) async-start(f32[32,1,64]{2,1,0:T(1,128)} %broadcast_in_dim.39), calls=%async_computation.3 | async-start | bytes 32768 | tf_op jit(solution)/shard_map/all_to_all | solution.py:22
  259.5 30.9 %copy-start.2 = (bf16[64,4096]{1,0:T(8,128)(2,1)S(1)}, bf16[64,4096]{1,0:T(8,128)(2,1)}, u32[]{:S(2)}) copy-start(bf16[64,4096]{1,0:T(8,128)(2,1)} %param.11) | copy-start | bytes 1572868
  261.7 26.8 %all-to-all-start.3 = ((f32[32,1,12352]{2,1,0:T(1,128)}), f32[32,1,12352]{2,1,0:T(1,128)S(1)}, u32[]{:S(2)}, u32[]{:S(2)}) async-start(f32[32,1,12352]{2,1,0:T(1,128)} %broadcast_in_dim.41), calls=%async_computation.4 | async-start | bytes 3178496 | tf_op jit(solution)/shard_map/all_to_all | solution.py:22
Sparse Core Ops, SparseCore 0:
  42.0 181.6 reduce-scatter.1
